TPU v7x, 512 devices: a whole 4x8x8 slice. The times are simulated.
512 devices in a mesh: feat: 64 (over x, z, core), node: 8 (over y).
Axes of the slice: x: 4, y: 8, z: 8, core: 2. Of those that a mesh axis runs over, the one named last changes fastest.
Arguments:
- feats: bfloat16 [1024, 131072], P('feat', 'node'), may hold values from -6 to 6
- weight: bfloat16 [1024, 256], replicated, may hold values from -0.1875 to 0.1875
- tile_row: int32 [64, 8, 32], P('feat', 'node'), may hold values from 0 to 1, as said below
- tile_col: int32 [64, 8, 32], P('feat', 'node'), may hold values from 0 to 15
- tile_block: int32 [64, 8, 32], P('feat', 'node'), may hold values from 0 to 31, each once within a row
- tile_count: int32 [64, 8], P('feat', 'node'), may hold values from 8 to 32, as said below
- edge_blocks: bfloat16 [64, 8, 32, 128, 128], P('feat', 'node'), may hold values from -0.1875 to 0.1875
- cotangent: bfloat16 [256, 131072], P(None, ('node', 'feat')), may hold values from -0.016479492 to 0.016479492
Outputs:
- act: bfloat16 [256, 131072], P(None, ('node', 'feat'))
- weight_grad: float32 [1024, 256], P(('feat', 'node'))
Inputs may be any that keep to these rules, and one draw needn't show every extreme that they name: Within one device block the pairs (tile_row, tile_col) of its 32 slots name every tile position once. Within one device block tile_block names each of its 32 blocks once. Slots s at or after tile_count of their block are unused; some block uses all 32 slots.
All inputs are finite; a program needn't handle non-finite values.
Results may differ from a plain program's by a relative error of at most 0.012.
Values may be sent and summed in bfloat16 or wider, within the bound.
A program may use at most 64 MiB of HBM per device.

v0:
```python
import jax
import jax.numpy as jnp
from jax import lax
from jax.sharding import PartitionSpec as P

root_half = 0.7071067811865476
inv_root_two_pi = 0.3989422804014327


def dense_adjacency(row_tile, col_tile, block_index, live_count, blocks, row_tiles, col_tiles):
    slot_total = row_tile.shape[0]
    tile_size = blocks.shape[-1]
    position = row_tile * col_tiles + col_tile
    places = jnp.arange(row_tiles * col_tiles, dtype=jnp.int32)
    active = jnp.arange(slot_total, dtype=jnp.int32) < live_count
    matches = (position[None, :] == places[:, None]) & active[None, :]
    chosen = jnp.sum(jnp.where(matches, block_index[None, :], 0), axis=1)
    filled = jnp.any(matches, axis=1)
    picked = jnp.take(blocks, chosen, axis=0) * filled[:, None, None].astype(blocks.dtype)
    layout = picked.reshape(row_tiles, col_tiles, tile_size, tile_size)
    return layout.transpose(0, 2, 1, 3).reshape(row_tiles * tile_size, col_tiles * tile_size)


def gelu_parts(preact):
    normal_cdf = 0.5 * (1.0 + lax.erf(preact * root_half))
    normal_pdf = jnp.exp(-0.5 * preact * preact) * inv_root_two_pi
    return (preact * normal_cdf, normal_cdf + preact * normal_pdf)


def two_part(values):
    upper = lax.optimization_barrier(values.astype(jnp.bfloat16))
    lower = (values - upper.astype(jnp.float32)).astype(jnp.bfloat16)
    return (upper, lower)


def split_dot(left, right, dims):
    left_hi, left_lo = two_part(left)
    total = lax.dot_general(left_hi, right, dims, preferred_element_type=jnp.float32)
    return total + lax.dot_general(left_lo, right, dims, preferred_element_type=jnp.float32)


def per_device(feats, weight, tile_row, tile_col, tile_block, tile_count, edge_blocks, cotangent):
    feat_devices = lax.axis_size("feat")
    part_width, shard_nodes = feats.shape
    own_rows = shard_nodes // feat_devices
    tile_size = edge_blocks.shape[-1]
    row_tiles = own_rows // tile_size
    slot_total = edge_blocks.shape[2]
    adjacency = dense_adjacency(
        tile_row[0, 0],
        tile_col[0, 0],
        tile_block[0, 0],
        tile_count[0, 0],
        edge_blocks[0, 0],
        row_tiles,
        slot_total // row_tiles,
    )
    by_dest = feats.reshape(part_width, feat_devices, own_rows)
    contract_last = (((1,), (1,)), ((), ()))
    contract_first = (((0,), (0,)), ((), ()))
    arrive_local_rows = lax.all_to_all(by_dest, "feat", split_axis=1, concat_axis=0, tiled=True)[
        :, 0, :
    ]
    projected = lax.dot_general(
        weight, arrive_local_rows, contract_first, preferred_element_type=jnp.float32
    )
    local_rows, projected = (arrive_local_rows, projected)
    columns = adjacency
    preact = split_dot(
        lax.all_gather(projected, "node", axis=1, tiled=True), columns, contract_last
    )
    output, derivative = gelu_parts(preact)
    pre_grad = cotangent.astype(jnp.float32) * derivative
    grad_hi, grad_lo = two_part(pre_grad)
    columns = adjacency
    total = lax.dot_general(
        columns, grad_hi, (((0,), (1,)), ((), ())), preferred_element_type=jnp.float32
    )
    node_grad = lax.psum_scatter(
        (
            total
            + lax.dot_general(
                columns, grad_lo, (((0,), (1,)), ((), ())), preferred_element_type=jnp.float32
            )
        ).astype(jnp.bfloat16),
        "node",
        scatter_dimension=0,
        tiled=True,
    ).astype(jnp.float32)
    node_hi, node_lo = two_part(node_grad)
    total = jnp.dot(local_rows, node_hi, preferred_element_type=jnp.float32)
    weight_grad = lax.psum_scatter(
        total + jnp.dot(local_rows, node_lo, preferred_element_type=jnp.float32),
        ("feat", "node"),
        scatter_dimension=0,
        tiled=True,
    )
    return (output.astype(jnp.bfloat16), weight_grad)


def solution(mesh):
    return jax.shard_map(
        per_device,
        mesh=mesh,
        in_specs=(
            P("feat", "node"),
            P(),
            P("feat", "node", None),
            P("feat", "node", None),
            P("feat", "node", None),
            P("feat", "node"),
            P("feat", "node", None, None, None),
            P(None, ("node", "feat")),
        ),
        out_specs=(P(None, ("node", "feat")), P(("feat", "node"), None)),
        check_vma=False,
    )
```

profile of v0, /device:TPU:1, one launch (start us, length us, event | category | flops | bytes accessed | tf_op | source)
XLA Modules:
  0.0 416.8 jit_solution(16985593902049402030)
XLA Ops:
  7.2 0.0 copy-start
  7.2 0.0 copy-start.3
  7.2 0.0 all-gather.2.cloned.1.call-start
  7.3 1.2 copy.48
  8.5 31.9 %all_to_all.15 = bf16[16,64,256]{2,0,1:T(8,128)(2,1)S(1)} all-to-all(bf16[16,64,256]{2,0,1:T(8,128)(2,1)S(1)} %bitcast.54), channel_id=1, replica_groups=mesh['feat'=64,'node'=8] {'feat'}, dimensions={1} | all-to-all | bytes 1048576 | tf_op jit(solution)/shard_map/all_to_all | solution.py:61
  40.4 0.0 copy-done.3
  40.4 1.0 fusion.23
  41.4 0.0 all-gather.2.cloned.1.call-update
  41.4 0.0 reduce-scatter.3.cloned.1.call-start
  42.2 0.1 select_reduce_fusion
  42.3 0.1 reduce_sum.14
  42.4 0.1 fusion.19
  42.5 0.1 reshape.62
  42.6 1.7 gather_fusion
  44.3 1.9 fusion.8
  46.2 31.5 %all-gather.2.cloned.1.call-done = f32[256,2048]{1,0:T(8,128)} async-done(((f32[256,256]{1,0:T(8,128)}), f32[256,2048]{1,0:T(8,128)}) %all-gather.2.cloned.1.call-update) | async-done | bytes 2097168 | tf_op jit(solution)/shard_map/all_gather | solution.py:70
  77.7 1.7 convert_element_type.48
  79.5 0.0 copy-start.2
  79.5 0.5 fusion.6
  80.0 1.1 copy-done.1
  81.1 1.3 fusion.22
  82.3 0.5 fusion.3
  82.9 1.6 fusion
  84.5 0.0 reduce-scatter.3.cloned.1.call-update
  84.5 0.0 all-reduce.3.cloned.1.call-start
  84.6 39.4 %reduce-scatter.3.cloned.1.call-done = bf16[256,256]{1,0:T(8,128)(2,1)} async-done(((bf16[2048,256]{1,0:T(8,128)(2,1)}), bf16[256,256]{1,0:T(8,128)(2,1)}) %reduce-scatter.3.cloned.1.call-update) | async-done | bytes 131088 | tf_op jit(solution)/shard_map/reduce_scatter | solution.py:79
  124.0 1.3 fusion.24
  125.2 2.3 fusion.1
  127.5 0.0 all-reduce.3.cloned.1.call-update
  127.6 281.1 %all-reduce.3.cloned.1.call-done = f32[1024,256]{0,1:T(8,128)} async-done(((f32[1024,256]{0,1:T(8,128)}), f32[1024,256]{0,1:T(8,128)}) %all-reduce.3.cloned.1.call-update) | async-done | bytes 1048592
  408.6 1.0 constant_dynamic-slice_fusion
  409.6 0.7 copy.21
  (15 shorter events, 0.1 us)
Async XLA Ops:
  7.2 35.4 %copy-start = (bf16[1,1,32,128,128]{4,3,2,1,0:T(8,128)(2,1)S(1)}, bf16[1,1,32,128,128]{4,3,2,1,0:T(8,128)(2,1)}, u32[]{:S(2)}) copy-start(bf16[1,1,32,128,128]{4,3,2,1,0:T(8,128)(2,1)} %param.14) | copy-start | bytes 3145732
  7.2 33.2 %copy-start.3 = (bf16[1024,256]{1,0:T(8,128)(2,1)S(1)}, bf16[1024,256]{1,0:T(8,128)(2,1)}, u32[]{:S(2)}) copy-start(bf16[1024,256]{1,0:T(8,128)(2,1)} %param.9) | copy-start | bytes 1572868
  7.2 34.9 %copy-start.6 = (s32[1,1,32]{2,1,0:T(1,128)S(1)}, s32[1,1,32]{2,1,0:T(1,128)}, u32[]{:S(2)}) copy-start(s32[1,1,32]{2,1,0:T(1,128)} %param.10) | copy-start | bytes 388
  7.2 34.9 %copy-start.5 = (s32[1,1,32]{2,1,0:T(1,128)S(1)}, s32[1,1,32]{2,1,0:T(1,128)}, u32[]{:S(2)}) copy-start(s32[1,1,32]{2,1,0:T(1,128)} %param.11) | copy-start | bytes 388
  7.2 35.0 %copy-start.4 = (s32[1,1,32]{2,1,0:T(1,128)S(1)}, s32[1,1,32]{2,1,0:T(1,128)}, u32[]{:S(2)}) copy-start(s32[1,1,32]{2,1,0:T(1,128)} %param.12) | copy-start | bytes 388
  7.2 70.5 %all-gather.2.cloned.1.call-start = ((), (), s32[]{:S(2)}) async-start(), calls=%async_computation.2 | async-start | bytes 2359296 | tf_op jit(solution)/shard_map/all_gather | solution.py:70
  41.4 82.5 %reduce-scatter.3.cloned.1.call-start = ((), (), s32[]{:S(2)}) async-start(), calls=%async_computation.3 | async-start | bytes 1179648 | tf_op jit(solution)/shard_map/reduce_scatter | solution.py:79
  79.5 1.6 copy-start.1
  79.5 1.6 copy-start.2
  84.5 324.1 %all-reduce.3.cloned.1.call-start = ((), (), s32[]{:S(2)}) async-start(), calls=%async_computation.4 | async-start | bytes 2097152
Sparse Core Ops, SparseCore 0:
  41.5 36.1 all-gather.1
  84.7 39.2 reduce-scatter.2
  129.0 279.5 all-reduce.2
where the time goes:
time: 417 us
  waiting for transfers between devices  352 us (84%)
  blocking collectives  31.9 us (8%)
  between operations  14.6 us (4%)
  matrix products  8.54 us (2%)
  local copies, waits for them, and re-layouts  5.79 us (1%)
    unnamed x4, waiting for transfers between devices  281 us
    reduce_scatter x1, waiting for transfers between devices, per_device(): lax.psum_scatter((total + lax.dot_general(columns, grad_lo, (((0,), (1,))...  39.4 us
    all_to_all x1, blocking collectives, per_device(): lax.all_to_all(by_dest, 'feat', split_axis=1, concat_axis=0, tiled=True)  31.9 us
    all_gather x1, waiting for transfers between devices, per_device(): lax.all_gather(projected, 'node', axis=1, tiled=True)  31.5 us
  transfers between devices with their start and end apart: 3, of which 3 were waited for; matrix products, arithmetic and copies ran while one was open for 1% of the time, Pallas kernels for 0%

commit v1 on v0

--- a/solution.py
+++ b/solution.py
@@ -66,9 +66,8 @@
     )
     local_rows, projected = (arrive_local_rows, projected)
     columns = adjacency
-    preact = split_dot(
-        lax.all_gather(projected, "node", axis=1, tiled=True), columns, contract_last
-    )
+    gathered = lax.all_gather(projected.astype(jnp.bfloat16), "node", axis=1, tiled=True)
+    preact = lax.dot_general(gathered, columns, contract_last, preferred_element_type=jnp.float32)
     output, derivative = gelu_parts(preact)
     pre_grad = cotangent.astype(jnp.float32) * derivative
     grad_hi, grad_lo = two_part(pre_grad)
@@ -89,12 +88,14 @@
     ).astype(jnp.float32)
     node_hi, node_lo = two_part(node_grad)
     total = jnp.dot(local_rows, node_hi, preferred_element_type=jnp.float32)
-    weight_grad = lax.psum_scatter(
-        total + jnp.dot(local_rows, node_lo, preferred_element_type=jnp.float32),
-        ("feat", "node"),
-        scatter_dimension=0,
-        tiled=True,
-    )
+    total = total + jnp.dot(local_rows, node_lo, preferred_element_type=jnp.float32)
+    terms = total.astype(jnp.bfloat16).reshape(feat_devices, part_width, -1)
+    terms = lax.all_to_all(terms, "feat", split_axis=0, concat_axis=0, tiled=True)
+    feat_sum = jnp.sum(terms.astype(jnp.float32), axis=0)
+    node_devices = lax.axis_size("node")
+    shares = feat_sum.reshape(node_devices, part_width // node_devices, -1)
+    shares = lax.all_to_all(shares, "node", split_axis=0, concat_axis=0, tiled=True)
+    weight_grad = jnp.sum(shares, axis=0)
     return (output.astype(jnp.bfloat16), weight_grad)
 
 

time: 417 us -> 175 us (0.42)
  waiting for transfers between devices: 352 us -> 70 us
  blocking collectives: 31.9 us -> 75.7 us
    unnamed x4 -> x2, waiting for transfers between devices: 281 us -> 0.03 us
    all_to_all x0 -> x2, blocking collectives: none -> 43.8 us  [the longest x1 33.1 us: per_device(): lax.all_to_all(terms, 'feat', split_axis=0, concat_axis=0, tiled=True)]
  transfers between devices with their start and end apart: 3 -> 2, of which waited for: 3 -> 2; matrix products, arithmetic and copies ran while one was open for 1% -> 2% of each run, Pallas kernels for 0% -> 0%
where the time goes in v1:
time: 175 us
  blocking collectives  75.7 us (43%)
  waiting for transfers between devices  70 us (40%)
  between operations  14.8 us (8%)
  matrix products  8.22 us (5%)
  local copies, waits for them, and re-layouts  3.31 us (2%)
  other arithmetic  2.87 us (2%)
    reduce_scatter x1, waiting for transfers between devices, per_device(): lax.psum_scatter((total + lax.dot_general(columns, grad_lo, (((0,), (1,))...  41 us
    all_to_all x1, blocking collectives, per_device(): lax.all_to_all(terms, 'feat', split_axis=0, concat_axis=0, tiled=True)  33.1 us
    all_to_all x1, blocking collectives, per_device(): lax.all_to_all(by_dest, 'feat', split_axis=1, concat_axis=0, tiled=True)  31.9 us
    all_gather x1, waiting for transfers between devices, per_device(): lax.all_gather(projected.astype(jnp.bfloat16), 'node', axis=1, tiled=True)  28.9 us
    all_to_all x1, blocking collectives, per_device(): lax.all_to_all(shares, 'node', split_axis=0, concat_axis=0, tiled=True)  10.7 us
  transfers between devices with their start and end apart: 2, of which 2 were waited for; matrix products, arithmetic and copies ran while one was open for 2% of the time, Pallas kernels for 0%

profile of v1, /device:TPU:1, one launch (start us, length us, event | category | flops | bytes accessed | tf_op | source)
XLA Modules:
  0.0 174.9 jit_solution(7514860330004148019)
XLA Ops:
  7.2 0.0 copy-start
  7.2 0.0 copy-start.3
  7.2 0.0 copy-start.4
  7.2 0.0 copy-start.5
  7.2 0.0 copy-start.2
  7.2 0.0 all-gather.2.cloned.1.call-start
  7.3 1.2 copy.46
  8.5 31.9 %all_to_all.25 = bf16[16,64,256]{2,0,1:T(8,128)(2,1)S(1)} all-to-all(bf16[16,64,256]{2,0,1:T(8,128)(2,1)S(1)} %bitcast.51), channel_id=1, replica_groups=mesh['feat'=64,'node'=8] {'feat'}, dimensions={1} | all-to-all | bytes 1048576 | tf_op jit(solution)/shard_map/all_to_all | solution.py:61
  40.4 1.0 convolution_convert_fusion
  41.4 0.0 all-gather.2.cloned.1.call-update
  41.4 0.0 reduce-scatter.2.cloned.1.call-start
  42.1 0.1 fusion.18
  42.3 0.1 reshape.70
  42.3 0.1 select_reduce_fusion
  42.5 0.1 reduce_sum.32
  42.6 0.0 copy-start.1
  42.6 1.7 gather_fusion
  44.3 1.9 %fusion.8 = bf16[2,16,128,128]{3,1,2,0:T(8,128)(2,1)S(1)} fusion(bf16[2,16,128,128]{3,2,1,0:T(8,128)(2,1)} %bitcast.49, pred[2,16]{1,0:T(4,128)(4,1)S(1)} %compare_and_fusion, bf16[2,16]{1,0:T(2,128)(2,1)S(1)} %reshape.70), kind=kLoop, calls=%fused_computation.13 | loop fusion | flops 1048576 | bytes 2097248 | tf_op jit(solution)/shard_map/mul | solution.py:19
  46.2 28.9 %all-gather.2.cloned.1.call-done = bf16[256,2048]{1,0:T(8,128)(2,1)} async-done(((bf16[256,256]{1,0:T(8,128)(2,1)}), bf16[256,2048]{1,0:T(8,128)(2,1)}) %all-gather.2.cloned.1.call-update) | async-done | bytes 1048592 | tf_op jit(solution)/shard_map/all_gather | solution.py:69
  75.1 0.0 copy-done.1
  75.1 2.4 %fusion.21 = (bf16[256,256]{1,0:T(8,128)(2,1)S(1)}, bf16[256,256]{1,0:T(8,128)(2,1)}, f32[256,256]{1,0:T(8,128)S(1)}) fusion(bf16[256,256]{1,0:T(8,128)(2,1)S(1)} %copy-done.1, bf16[256,2048]{1,0:T(8,128)(2,1)} %all-gather.2.cloned.1.call-done, bf16[32,8,16,128]{3,2,1,0:T(8,128)(2,1)S(1)} %bitcast.43), kind=kOutput, calls=%fused_computation.40 | convolution fusion | flops 269287424 | bytes 2752512 | tf_op jit(solution)/shard_map/dot_general | solution.py:70
  77.5 0.5 fusion.4
  78.1 1.7 fusion
  79.7 0.0 reduce-scatter.2.cloned.1.call-update
  79.8 41.0 %reduce-scatter.2.cloned.1.call-done = bf16[256,256]{1,0:T(8,128)(2,1)} async-done(((bf16[2048,256]{1,0:T(8,128)(2,1)}), bf16[256,256]{1,0:T(8,128)(2,1)}) %reduce-scatter.2.cloned.1.call-update) | async-done | bytes 131088 | tf_op jit(solution)/shard_map/reduce_scatter | solution.py:78
  120.8 1.2 fusion.22
  122.1 1.3 fusion.2
  123.4 0.2 copy.23
  123.6 33.1 %all_to_all.26 = bf16[64,16,256]{2,1,0:T(8,128)(2,1)S(1)} all-to-all(bf16[64,16,256]{2,1,0:T(8,128)(2,1)S(1)} %bitcast.50), channel_id=1, replica_groups=mesh['feat'=64,'node'=8] {'feat'}, dimensions={0} | all-to-all | bytes 1048576 | tf_op jit(solution)/shard_map/all_to_all | solution.py:93
  156.7 0.1 convert_reduce_fusion
  156.8 10.7 %all_to_all.27 = f32[8,2,256]{2,1,0:T(2,128)S(1)} all-to-all(f32[8,2,256]{2,1,0:T(2,128)S(1)} %reshape.69), channel_id=1, replica_groups=mesh['feat'=64,'node'=8] {'node'}, dimensions={0} | all-to-all | bytes 32768 | tf_op jit(solution)/shard_map/all_to_all | solution.py:97
  167.5 0.6 reduce_sum.35
  (12 shorter events, 0.1 us)
Async XLA Ops:
  7.2 35.4 %copy-start = (bf16[1,1,32,128,128]{4,3,2,1,0:T(8,128)(2,1)S(1)}, bf16[1,1,32,128,128]{4,3,2,1,0:T(8,128)(2,1)}, u32[]{:S(2)}) copy-start(bf16[1,1,32,128,128]{4,3,2,1,0:T(8,128)(2,1)} %param.14) | copy-start | bytes 3145732
  7.2 33.2 %copy-start.3 = (bf16[1024,256]{1,0:T(8,128)(2,1)S(1)}, bf16[1024,256]{1,0:T(8,128)(2,1)}, u32[]{:S(2)}) copy-start(bf16[1024,256]{1,0:T(8,128)(2,1)} %param.9) | copy-start | bytes 1572868
  7.2 34.9 %copy-start.4 = (s32[1,1,32]{2,1,0:T(1,128)S(1)}, s32[1,1,32]{2,1,0:T(1,128)}, u32[]{:S(2)}) copy-start(s32[1,1,32]{2,1,0:T(1,128)} %param.11) | copy-start | bytes 388
  7.2 34.9 %copy-start.5 = (s32[1,1,32]{2,1,0:T(1,128)S(1)}, s32[1,1,32]{2,1,0:T(1,128)}, u32[]{:S(2)}) copy-start(s32[1,1,32]{2,1,0:T(1,128)} %param.10) | copy-start | bytes 388
  7.2 35.1 %copy-start.2 = (s32[1,1,32]{2,1,0:T(1,128)S(1)}, s32[1,1,32]{2,1,0:T(1,128)}, u32[]{:S(2)}) copy-start(s32[1,1,32]{2,1,0:T(1,128)} %param.12) | copy-start | bytes 388
  7.2 67.9 %all-gather.2.cloned.1.call-start = ((), (), s32[]{:S(2)}) async-start(), calls=%async_computation.4 | async-start | bytes 1179648 | tf_op jit(solution)/shard_map/all_gather | solution.py:69
  41.4 79.4 %reduce-scatter.2.cloned.1.call-start = ((), (), s32[]{:S(2)}) async-start(), calls=%async_computation.5 | async-start | bytes 1179648 | tf_op jit(solution)/shard_map/reduce_scatter | solution.py:78
  42.6 32.5 %copy-start.1 = (bf16[256,256]{1,0:T(8,128)(2,1)S(1)}, bf16[256,256]{1,0:T(8,128)(2,1)}, u32[]{:S(2)}) copy-start(bf16[256,256]{1,0:T(8,128)(2,1)} %param.15) | copy-start | bytes 393220
Sparse Core Ops, SparseCore 0:
  41.5 33.5 all-gather.1
  79.9 40.8 reduce-scatter.1

commit v2 on v0

v2 whole, which is shorter than its diff:
```python
import functools

import jax
import jax.numpy as jnp
from jax import lax
from jax.experimental import pallas as pl
from jax.experimental.pallas import tpu as pltpu
from jax.sharding import PartitionSpec as P

MESH = pl.DeviceIdType.MESH
root_half = 0.7071067811865476
inv_root_two_pi = 0.3989422804014327
RIGHT, LEFT = 0, 1
UPTO = 9
NH = 2
NEAR = (((1,), (1,)), ((), ()))
PLAIN = (((1,), (0,)), ((), ()))


def dot(left, right, dims):
    return lax.dot_general(left, right, dims, preferred_element_type=jnp.float32)


def kernel(
    nf, nn, row_ref, col_ref, blk_ref, cnt_ref, feats, weight, edges, cot, act, wgrad,
    edges_v, weight_v, cot_v, wt, adj, x, p, acc, pg, rs_out, rs_in, ng, wg_out, wg_in,
    ys, y_in, local_sem, x_recv, x_send, ag_send, ag_recv, rs_send, rs_recv,
    wg_send, wg_recv, y_send, y_recv,
):
    f, n = lax.axis_index("feat"), lax.axis_index("node")
    part = feats.shape[0]
    half = x.shape[2]
    own = 2 * half
    hid = acc.shape[0]
    hp_rows = hid // NH
    right, left = lax.rem(n + 1, nn), lax.rem(n + nn - 1, nn)

    loads = [
        pltpu.make_async_copy(edges.at[0, 0], edges_v, local_sem.at[0]),
        pltpu.make_async_copy(weight, weight_v, local_sem.at[1]),
        pltpu.make_async_copy(cot, cot_v, local_sem.at[2]),
    ]
    for copy in loads:
        copy.start()

    barrier = pltpu.get_barrier_semaphore()

    def greet_feat(i, carry):
        pl.semaphore_signal(barrier, inc=1, device_id=(lax.rem(f + i, nf), n), device_id_type=MESH)
        return carry

    def greet_node(i, carry):
        pl.semaphore_signal(barrier, inc=1, device_id=(f, lax.rem(n + i, nn)), device_id_type=MESH)
        return carry

    lax.fori_loop(1, nf, greet_feat, 0)
    lax.fori_loop(1, nn, greet_node, 0)

    own_loads = []
    for a in range(2):
        copy = pltpu.make_async_copy(
            feats.at[:, pl.ds(pl.multiple_of(f * own + a * half, half), half)],
            x.at[a, pl.ds(pl.multiple_of(f * part, part), part)],
            local_sem.at[3 + a],
        )
        copy.start()
        own_loads.append(copy)

    pl.semaphore_wait(barrier, nf + nn - 2)

    def feat_copy(a, i):
        to = lax.rem(f + i, nf)
        return pltpu.make_async_remote_copy(
            src_ref=feats.at[:, pl.ds(pl.multiple_of(to * own + a * half, half), half)],
            dst_ref=x.at[a, pl.ds(pl.multiple_of(f * part, part), part)],
            send_sem=x_send.at[a],
            recv_sem=x_recv.at[a],
            device_id=(to, n),
            device_id_type=MESH,
        )

    for a in range(2):

        def send_feat(i, carry):
            feat_copy(a, i).start()
            return carry

        lax.fori_loop(1, nf, send_feat, 0)

    def all_feats(a):
        block = x.at[a, pl.ds(0, (nf - 1) * part)]
        return pltpu.make_async_remote_copy(
            src_ref=block, dst_ref=block, send_sem=x_send.at[a], recv_sem=x_recv.at[a],
            device_id=(f, n), device_id_type=MESH,
        )

    loads[1].wait()
    wt[...] = weight_v[...].T
    loads[0].wait()
    slots = edges_v.shape[0]
    cols = 2 * nn
    count = cnt_ref[0, 0]
    for r in range(2):

        def place(c, carry):
            chosen, used = jnp.int32(0), jnp.int32(0)
            for s in range(slots):
                hit = jnp.logical_and(row_ref[0, 0, s] == r, col_ref[0, 0, s] == c)
                hit = jnp.logical_and(hit, s < count)
                chosen = chosen + jnp.where(hit, blk_ref[0, 0, s], 0)
                used = used + jnp.where(hit, 1, 0)
            block = edges_v[chosen].astype(jnp.float32)
            block = jnp.where(used > 0, block, 0.0)
            adj[c, pl.ds(r * half, half), :] = block.astype(jnp.bfloat16)
            return carry

        lax.fori_loop(0, cols, place, 0)
    loads[2].wait()

    finals = []

    def ag_len(d, a, h):
        longer = (a + h) % 2 == 0
        return 4 if longer == (d == RIGHT) else 3

    def rows_of(h):
        return pl.ds(h * hp_rows, hp_rows)

    def ag_copy(d, s, a, h, slot):
        block = p.at[slot, a, rows_of(h)]
        return pltpu.make_async_remote_copy(
            src_ref=block, dst_ref=block,
            send_sem=ag_send.at[d, s, a, h], recv_sem=ag_recv.at[d, s, a, h],
            device_id=(f, right if d == RIGHT else left), device_id_type=MESH,
        )

    def slot_at(d, s):
        return lax.rem(n + nn - s, nn) if d == RIGHT else lax.rem(n + s, nn)

    def ag_send_step(d, s, a, h):
        copy = ag_copy(d, s, a, h, slot_at(d, s))
        copy.start()
        finals.append(copy.wait_send)

    def add_block(slot, a, h, first):
        term = dot(p[slot, a, rows_of(h), :], adj[2 * slot + a], NEAR)
        if first:
            acc[rows_of(h), :] = term
        else:
            acc[rows_of(h), :] += term

    def project(a):
        all_feats(a).wait_recv()
        own_loads[a].wait()
        p[n, a] = dot(wt[...], x[a], PLAIN).astype(jnp.bfloat16)
        for h in range(NH):
            for d in (RIGHT, LEFT):
                ag_send_step(d, 0, a, h)
        for h in range(NH):
            add_block(n, a, h, a == 0)

    def ag_step(s, a, h):
        got = []
        for d in (RIGHT, LEFT):
            if s <= ag_len(d, a, h):
                ag_copy(d, s - 1, a, h, slot_at(d, s)).wait_recv()
                got.append(d)
                if s < ag_len(d, a, h):
                    ag_send_step(d, s, a, h)
        for d in got:
            add_block(slot_at(d, s), a, h, False)

    def activate(h):
        u = acc[rows_of(h), :]
        cdf = 0.5 * (1.0 + lax.erf(u * root_half))
        pdf = jnp.exp(-0.5 * u * u) * inv_root_two_pi
        act[rows_of(h), :] = (u * cdf).astype(jnp.bfloat16)
        grad = cot_v[rows_of(h), :].astype(jnp.float32) * (cdf + u * pdf)
        pg[rows_of(h), :] = grad.astype(jnp.bfloat16)

    def rs_len(d, h):
        return 4 if (h % 2 == 0) == (d == RIGHT) else 3

    def rs_copy(d, s, h):
        return pltpu.make_async_remote_copy(
            src_ref=rs_out.at[d, s, rows_of(h)], dst_ref=rs_in.at[d, s, rows_of(h)],
            send_sem=rs_send.at[d, s, h], recv_sem=rs_recv.at[d, s, h],
            device_id=(f, right if d == RIGHT else left), device_id_type=MESH,
        )

    def term(m, h):
        block = jnp.concatenate([adj[2 * m], adj[2 * m + 1]], axis=1)
        return dot(pg[rows_of(h), :], block, PLAIN)

    def rs_step(s, h):
        for d in (RIGHT, LEFT):
            away = rs_len(d, h) - s
            if away <= 0:
                continue
            m = lax.rem(n + away, nn) if d == RIGHT else lax.rem(n + nn - away, nn)
            total = term(m, h)
            if s > 0:
                rs_copy(d, s - 1, h).wait_recv()
                total = total + rs_in[d, s - 1, rows_of(h), :].astype(jnp.float32)
            rs_out[d, s, rows_of(h), :] = total.astype(jnp.bfloat16)
            copy = rs_copy(d, s, h)
            copy.start()
            finals.append(copy.wait_send)

    def rs_end(h):
        total = term(n, h)
        for d in (RIGHT, LEFT):
            rs_copy(d, rs_len(d, h) - 1, h).wait_recv()
            total = total + rs_in[d, rs_len(d, h) - 1, rows_of(h), :].astype(jnp.float32)
        ng[rows_of(h), :] = total.astype(jnp.bfloat16)

    def wg_copy(w, i):
        to = lax.rem(f + i, nf)
        return pltpu.make_async_remote_copy(
            src_ref=wg_out.at[w, to], dst_ref=wg_in.at[w, f],
            send_sem=wg_send.at[w], recv_sem=wg_recv.at[w],
            device_id=(to, n), device_id_type=MESH,
        )

    def wg_all(w):
        block = wg_in.at[w, pl.ds(0, nf - 1)]
        return pltpu.make_async_remote_copy(
            src_ref=block, dst_ref=block, send_sem=wg_send.at[w], recv_sem=wg_recv.at[w],
            device_id=(f, n), device_id_type=MESH,
        )

    def wg_start(w):
        units = pl.ds(w * 128, 128)
        quarter = nf // 4
        for q in range(4):
            features = pl.ds(q * quarter * part, quarter * part)
            block = dot(x[0, features, :], ng[units, pl.ds(0, half)], NEAR)
            block = block + dot(x[1, features, :], ng[units, pl.ds(half, half)], NEAR)
            wg_out[w, pl.ds(q * quarter, quarter)] = block.astype(jnp.bfloat16).reshape(quarter, part, 128)

        def send_wg(i, carry):
            wg_copy(w, i).start()
            return carry

        lax.fori_loop(1, nf, send_wg, 0)
        wg_in[w, f] = wg_out[w, f]

    def y_copy(w, i):
        to = lax.rem(n + i, nn)
        return pltpu.make_async_remote_copy(
            src_ref=ys.at[w, lax.div(to, 4)], dst_ref=y_in.at[w, n],
            send_sem=y_send.at[w], recv_sem=y_recv.at[w],
            device_id=(f, to), device_id_type=MESH,
        )

    def y_all(w):
        block = y_in.at[w, pl.ds(0, nn - 1)]
        return pltpu.make_async_remote_copy(
            src_ref=block, dst_ref=block, send_sem=y_send.at[w], recv_sem=y_recv.at[w],
            device_id=(f, n), device_id_type=MESH,
        )

    def wg_sum(w):
        wg_all(w).wait_recv()
        total = jnp.sum(wg_in[w].astype(jnp.float32), axis=0)
        ys[w] = total.reshape(2, 8, 128)

        def send_y(i, carry):
            y_copy(w, i).start()
            return carry

        lax.fori_loop(1, nn, send_y, 0)
        y_in[w, n] = ys[w, lax.div(n, 4)]

    def y_sum(w):
        y_all(w).wait_recv()
        total = jnp.sum(y_in[w], axis=0)
        at = lax.rem(n, 4)
        mine = total[6:8]
        for k in range(3):
            mine = jnp.where(at == k, total[2 * k : 2 * k + 2], mine)
        wgrad[:, pl.ds(w * 128, 128)] = mine

    halves = range(NH)
    if UPTO == 1:
        for a in range(2):
            all_feats(a).wait_recv()
            own_loads[a].wait()
        act[...] = x[0, 0:256, :].astype(jnp.bfloat16).repeat(2, axis=1) if False else cot_v[...]
        wgrad[...] = jnp.zeros_like(wgrad)
    if UPTO >= 2:
        project(0)
        for s in (1, 2):
            for h in halves:
                ag_step(s, 0, h)
        project(1)
        for h in halves:
            ag_step(3, 0, h)
        for h in halves:
            ag_step(1, 1, h)
        for h in halves:
            ag_step(4, 0, h)
        for s in (2, 3, 4):
            for h in halves:
                ag_step(s, 1, h)
                if s == 4:
                    activate(h)
                    if UPTO >= 3:
                        rs_step(0, h)
        if UPTO == 2:
            wgrad[...] = jnp.zeros_like(wgrad)
    if UPTO >= 3:
        for s in (1, 2, 3):
            for h in halves:
                rs_step(s, h)
        if UPTO == 3:
            for h in halves:
                rs_end(h)
            wgrad[...] = jnp.zeros_like(wgrad)
    if UPTO >= 4:
        for w in range(2):
            for h in range(w * NH // 2, (w + 1) * NH // 2):
                rs_end(h)
            wg_start(w)
        for w in range(2):
            wg_sum(w)
        for w in range(2):
            y_sum(w)
            wg_all(w).wait_send()
            y_all(w).wait_send()
    for a in range(2):
        all_feats(a).wait_send()
    for wait in finals:
        wait()


def per_device(nf, nn, feats, weight, tile_row, tile_col, tile_block, tile_count, edge_blocks, cotangent):
    fin, hid = weight.shape
    own = cotangent.shape[1]
    half = own // 2
    part = feats.shape[0]
    slots = edge_blocks.shape[2]
    bf, f32 = jnp.bfloat16, jnp.float32
    vm, dma = pltpu.VMEM, pltpu.SemaphoreType.DMA
    smem = pl.BlockSpec(memory_space=pltpu.SMEM)
    anywhere = pl.BlockSpec(memory_space=pl.ANY)
    return pl.pallas_call(
        functools.partial(kernel, nf, nn),
        out_shape=(
            jax.ShapeDtypeStruct((hid, own), bf),
            jax.ShapeDtypeStruct((fin // (nf * nn), hid), f32),
        ),
        in_specs=[smem] * 4 + [anywhere] * 4,
        out_specs=(pl.BlockSpec(memory_space=vm), pl.BlockSpec(memory_space=vm)),
        scratch_shapes=[
            vm((slots, half, half), bf),
            vm((fin, hid), bf),
            vm((hid, own), bf),
            vm((hid, fin), bf),
            vm((2 * nn, own, half), bf),
            vm((2, fin, half), bf),
            vm((nn, 2, hid, half), bf),
            vm((hid, own), f32),
            vm((hid, own), bf),
            vm((2, 4, hid, own), bf),
            vm((2, 4, hid, own), bf),
            vm((hid, own), bf),
            vm((2, nf, part, 128), bf),
            vm((2, nf, part, 128), bf),
            vm((2, 2, 8, 128), f32),
            vm((2, nn, 8, 128), f32),
            dma((5,)),
            dma((2,)),
            dma((2,)),
            dma((2, 4, 2, NH)),
            dma((2, 4, 2, NH)),
            dma((2, 4, NH)),
            dma((2, 4, NH)),
            dma((2,)),
            dma((2,)),
            dma((2,)),
            dma((2,)),
        ],
        compiler_params=pltpu.CompilerParams(
            collective_id=0, has_side_effects=True, vmem_limit_bytes=40 * 1024 * 1024
        ),
        name="graphconv",
    )(tile_row, tile_col, tile_block, tile_count, feats, weight, edge_blocks, cotangent)


def solution(mesh):
    return jax.shard_map(
        functools.partial(per_device, mesh.shape["feat"], mesh.shape["node"]),
        mesh=mesh,
        in_specs=(
            P("feat", "node"),
            P(),
            P("feat", "node", None),
            P("feat", "node", None),
            P("feat", "node", None),
            P("feat", "node"),
            P("feat", "node", None, None, None),
            P(None, ("node", "feat")),
        ),
        out_specs=(P(None, ("node", "feat")), P(("feat", "node"), None)),
        check_vma=False,
    )
```

time: 417 us -> 86.7 us (0.21)
  waiting for transfers between devices: 352 us -> 0 us
  Pallas kernels: 0 us -> 79.6 us
  blocking collectives: 31.9 us -> 0 us
  between operations: 14.6 us -> 1.37 us
  matrix products: 8.54 us -> 0 us
    unnamed x4 -> x0, waiting for transfers between devices: 281 us -> none
    pallas_call x0 -> x1, Pallas kernels: none -> 79.6 us  [per_device(): pl.pallas_call(functools.partial(kernel, nf, nn), out_shape=(jax.ShapeDty...]
    reduce_scatter x1 -> x0, waiting for transfers between devices: 39.4 us -> none  [per_device(): lax.psum_scatter((total + lax.dot_general(columns, grad_lo, (((0,), (1,))...]
    all_to_all x1 -> x0, blocking collectives: 31.9 us -> none  [per_device(): lax.all_to_all(by_dest, 'feat', split_axis=1, concat_axis=0, tiled=True)]
    all_gather x1 -> x0, waiting for transfers between devices: 31.5 us -> none  [per_device(): lax.all_gather(projected, 'node', axis=1, tiled=True)]
    dot_general x7 -> x0, matrix products: 8.54 us -> none  [the longest x1 2.31 us: per_device(): jnp.dot(local_rows, node_lo, preferred_element_type=jnp.float32)]
  transfers between devices with their start and end apart: 3 -> 0, of which waited for: 3 -> 0; matrix products, arithmetic and copies ran while one was open for 1% -> 0% of each run, Pallas kernels for 0% -> 0%
where the time goes in v2:
time: 86.7 us; the launch traced here: 86.4 us
  Pallas kernels  79.6 us (92%)
  local copies, waits for them, and re-layouts  5.45 us (6%)
  between operations  1.37 us (2%)
    pallas_call x1, Pallas kernels, per_device(): pl.pallas_call(functools.partial(kernel, nf, nn), out_shape=(jax.ShapeDty...  79.6 us
    unnamed x16, local copies, waits for them, and re-layouts  5.45 us

profile of v2, /device:TPU:1, one launch (start us, length us, event | category | flops | bytes accessed | tf_op | source)
XLA Modules:
  0.0 86.4 jit_solution(14606784190423861617)
XLA Ops:
  0.6 0.0 copy-start.6
  0.6 0.0 copy-start.5
  0.7 0.0 copy-start.4
  1.3 0.0 copy-done.6
  1.3 0.0 copy-done.5
  1.4 0.0 copy-done.4
  1.4 0.0 copy-start
  1.4 1.2 %copy-done = bf16[1,1,32,128,128]{4,3,2,1,0:T(8,128)(2,1)S(1)} copy-done((bf16[1,1,32,128,128]{4,3,2,1,0:T(8,128)(2,1)S(1)}, bf16[1,1,32,128,128]{4,3,2,1,0:T(8,128)(2,1)}, u32[]{:S(2)}) %copy-start) | copy-done | bytes 1048600
  2.6 0.0 copy-start.1
  2.6 1.0 %copy-done.1 = bf16[16,16384]{1,0:T(8,128)(2,1)S(1)} copy-done((bf16[16,16384]{1,0:T(8,128)(2,1)S(1)}, bf16[16,16384]{1,0:T(8,128)(2,1)}, u32[]{:S(2)}) %copy-start.1) | copy-done | bytes 524312
  3.6 0.0 copy-start.2
  3.6 1.0 %copy-done.2 = bf16[1024,256]{1,0:T(8,128)(2,1)S(1)} copy-done((bf16[1024,256]{1,0:T(8,128)(2,1)S(1)}, bf16[1024,256]{1,0:T(8,128)(2,1)}, u32[]{:S(2)}) %copy-start.2) | copy-done | bytes 524312
  4.7 0.0 copy-start.3
  4.7 0.9 %copy-done.3 = bf16[256,256]{1,0:T(8,128)(2,1)S(1)} copy-done((bf16[256,256]{1,0:T(8,128)(2,1)S(1)}, bf16[256,256]{1,0:T(8,128)(2,1)}, u32[]{:S(2)}) %copy-start.3) | copy-done | bytes 131096
  5.6 79.6 %graphconv.1 = (bf16[256,256]{1,0:T(8,128)(2,1)S(1)}, f32[2,256]{1,0:T(2,128)S(1)}) custom-call(s32[1,1,32]{2,1,0:T(1,128)S(1)} %copy-done.4, s32[1,1,32]{2,1,0:T(1,128)S(1)} %copy-done.5, s32[1,1,32]{2,1,0:T(1,128)S(1)} %copy-done.6, s32[1,1]{1,0:T(1,128)S(6)} %copy.12.cnt_ref, bf16[16,16384]{1,0:T(8,128)(2,1)S(1)} %copy-done.1, ...), custom_call_target="tpu_custom_call" | custom-call | tf_op jit(solution)/shard_map/graphconv/pallas_call | solution.py:347
  85.1 0.7 copy.13
  85.8 0.6 copy.14
Async XLA Ops:
  0.6 0.7 copy-start.6
  0.6 0.7 copy-start.5
  0.7 0.7 copy-start.4
  1.4 1.2 %copy-start = (bf16[1,1,32,128,128]{4,3,2,1,0:T(8,128)(2,1)S(1)}, bf16[1,1,32,128,128]{4,3,2,1,0:T(8,128)(2,1)}, u32[]{:S(2)}) copy-start(bf16[1,1,32,128,128]{4,3,2,1,0:T(8,128)(2,1)} %edges.1) | copy-start | bytes 3145732
  2.6 1.0 %copy-start.1 = (bf16[16,16384]{1,0:T(8,128)(2,1)S(1)}, bf16[16,16384]{1,0:T(8,128)(2,1)}, u32[]{:S(2)}) copy-start(bf16[16,16384]{1,0:T(8,128)(2,1)} %feats.1) | copy-start | bytes 1572868
  3.6 1.0 %copy-start.2 = (bf16[1024,256]{1,0:T(8,128)(2,1)S(1)}, bf16[1024,256]{1,0:T(8,128)(2,1)}, u32[]{:S(2)}) copy-start(bf16[1024,256]{1,0:T(8,128)(2,1)} %weight.1) | copy-start | bytes 1572868
  4.7 0.9 %copy-start.3 = (bf16[256,256]{1,0:T(8,128)(2,1)S(1)}, bf16[256,256]{1,0:T(8,128)(2,1)}, u32[]{:S(2)}) copy-start(bf16[256,256]{1,0:T(8,128)(2,1)} %cot.1) | copy-start | bytes 393220

commit v3 on v2

v3 whole, which is shorter than its diff:
```python
import functools

import jax
import jax.numpy as jnp
from jax import lax
from jax.experimental import pallas as pl
from jax.experimental.pallas import tpu as pltpu
from jax.sharding import PartitionSpec as P

MESH = pl.DeviceIdType.MESH
root_half = 0.7071067811865476
inv_root_two_pi = 0.3989422804014327
RIGHT, LEFT = 0, 1
NH = 4
ORDER = (2, 1, 3, 4)
AG_TREE = {1: 0, 2: 0, 3: 2, 4: 2}
RS_TREE = {1: 0, 2: 1, 3: 2, 4: 2}
NEAR = (((1,), (1,)), ((), ()))
PLAIN = (((1,), (0,)), ((), ()))


def dot(left, right, dims):
    return lax.dot_general(left, right, dims, preferred_element_type=jnp.float32)


def kernel(
    nf, nn, row_any, col_any, blk_any, cnt_ref, feats, weight, edges, cot, act, wgrad,
    row_ref, col_ref, blk_ref, edges_v, weight_v, cot_v, feats_v, fs, wt, adj, x, p, acc, pg,
    rs_out, rs_in, ng, wg_out, wg_in, ys, y_in, local_sem, x_recv, x_send, ag_send, ag_recv, rs_send,
    rs_recv, wg_send, wg_recv, y_send, y_recv,
):
    f, n = lax.axis_index("feat"), lax.axis_index("node")
    part = feats.shape[0]
    half = x.shape[2]
    own = 2 * half
    hid = acc.shape[0]
    hp_rows = hid // NH
    right, left = lax.rem(n + 1, nn), lax.rem(n + nn - 1, nn)

    nz = nn
    fx, fz, fc = lax.div(f, 2 * nz), lax.rem(lax.div(f, 2), nz), lax.rem(f, 2)
    group = 2 * fx + fc
    groups = nf // nz

    def feat_of(g, z):
        return lax.div(g, 2) * (2 * nz) + z * 2 + lax.rem(g, 2)

    loads = [
        pltpu.make_async_copy(feats, feats_v, local_sem.at[3]),
        pltpu.make_async_copy(weight, weight_v, local_sem.at[1]),
        pltpu.make_async_copy(edges.at[0, 0], edges_v, local_sem.at[0]),
        pltpu.make_async_copy(cot, cot_v, local_sem.at[2]),
        pltpu.make_async_copy(row_any, row_ref, local_sem.at[4]),
        pltpu.make_async_copy(col_any, col_ref, local_sem.at[5]),
        pltpu.make_async_copy(blk_any, blk_ref, local_sem.at[6]),
    ]
    for copy in loads:
        copy.start()

    barrier = pltpu.get_barrier_semaphore()

    def greet_feat(i, carry):
        pl.semaphore_signal(barrier, inc=1, device_id=(lax.rem(f + i, nf), n), device_id_type=MESH)
        return carry

    def greet_node(i, carry):
        z = lax.rem(i, nz)
        to = lax.rem(n + lax.div(i, nz), nn)
        pl.semaphore_signal(barrier, inc=1, device_id=(feat_of(group, z), to), device_id_type=MESH)
        return carry

    lax.fori_loop(1, nf, greet_feat, 0)
    lax.fori_loop(nz, nz * nn, greet_node, 0)

    loads[0].wait()

    def spread(t, carry):
        for a in range(2):
            fs[a, t] = feats_v[:, pl.ds(pl.multiple_of(t * own + a * half, half), half)]
        return carry

    lax.fori_loop(0, nf, spread, 0)
    for a in range(2):
        x[a, pl.ds(pl.multiple_of(f * part, part), part), :] = fs[a, f]

    pl.semaphore_wait(barrier, nf - 1 + nz * (nn - 1))

    def feat_copy(a, i):
        to = lax.rem(f + i, nf)
        return pltpu.make_async_remote_copy(
            src_ref=fs.at[a, to],
            dst_ref=x.at[a, pl.ds(pl.multiple_of(f * part, part), part)],
            send_sem=x_send.at[a],
            recv_sem=x_recv.at[a],
            device_id=(to, n),
            device_id_type=MESH,
        )

    for a in range(2):

        def send_feat(i, carry):
            feat_copy(a, i).start()
            return carry

        lax.fori_loop(1, nf, send_feat, 0)

    def all_feats(a):
        block = x.at[a, pl.ds(0, (nf - 1) * part)]
        return pltpu.make_async_remote_copy(
            src_ref=block, dst_ref=block, send_sem=x_send.at[a], recv_sem=x_recv.at[a],
            device_id=(f, n), device_id_type=MESH,
        )

    loads[1].wait()
    wt[...] = weight_v[...].T
    for k in (2, 4, 5, 6):
        loads[k].wait()
    slots = edges_v.shape[0]
    cols = 2 * nn
    count = cnt_ref[0, 0]
    for r in range(2):

        def place(c, carry):
            chosen, used = jnp.int32(0), jnp.int32(0)
            for s in range(slots):
                hit = jnp.logical_and(row_ref[0, 0, s] == r, col_ref[0, 0, s] == c)
                hit = jnp.logical_and(hit, s < count)
                chosen = chosen + jnp.where(hit, blk_ref[0, 0, s], 0)
                used = used + jnp.where(hit, 1, 0)
            block = edges_v[chosen].astype(jnp.float32)
            block = jnp.where(used > 0, block, 0.0)
            adj[c, pl.ds(r * half, half), :] = block.astype(jnp.bfloat16)
            return carry

        lax.fori_loop(0, cols, place, 0)
    loads[3].wait()

    finals = []

    def ag_len(d, a, h):
        longer = (a + h) % 2 == 0
        return 4 if longer == (d == RIGHT) else 3

    def rows_of(h):
        return pl.ds(h * hp_rows, hp_rows)

    def slot_at(d, s):
        return lax.rem(n + nn - s, nn) if d == RIGHT else lax.rem(n + s, nn)

    def to_node(d, hop):
        return lax.rem(n + hop, nn) if d == RIGHT else lax.rem(n + nn - hop, nn)

    def ag_copy(d, at, hop, a, h):
        block = p.at[slot_at(d, at), a, rows_of(h)]
        return pltpu.make_async_remote_copy(
            src_ref=block, dst_ref=block,
            send_sem=ag_send.at[d, at + hop - 1, a, h], recv_sem=ag_recv.at[d, at + hop - 1, a, h],
            device_id=(f, to_node(d, hop)), device_id_type=MESH,
        )

    def ag_pass(d, at, a, h):
        for k in sorted(AG_TREE, reverse=True):
            if AG_TREE[k] == at and k <= ag_len(d, a, h):
                copy = ag_copy(d, at, k - at, a, h)
                copy.start()
                finals.append(copy.wait_send)

    def add_block(slot, a, h, first):
        term = dot(p[slot, a, rows_of(h), :], adj[2 * slot + a], NEAR)
        if first:
            acc[rows_of(h), :] = term
        else:
            acc[rows_of(h), :] += term

    def project(a):
        all_feats(a).wait_recv()
        p[n, a] = dot(wt[...], x[a], PLAIN).astype(jnp.bfloat16)
        for h in range(NH):
            for d in (RIGHT, LEFT):
                ag_pass(d, 0, a, h)
        for h in range(NH):
            add_block(n, a, h, a == 0)

    def ag_step(k, a, h):
        got = [d for d in (RIGHT, LEFT) if k <= ag_len(d, a, h)]
        for d in got:
            block = p.at[slot_at(d, k), a, rows_of(h)]
            pltpu.make_async_remote_copy(
                src_ref=block, dst_ref=block,
                send_sem=ag_send.at[d, k - 1, a, h], recv_sem=ag_recv.at[d, k - 1, a, h],
                device_id=(f, n), device_id_type=MESH,
            ).wait_recv()
            ag_pass(d, k, a, h)
        for d in got:
            add_block(slot_at(d, k), a, h, False)

    def activate(h):
        u = acc[rows_of(h), :]
        cdf = 0.5 * (1.0 + lax.erf(u * root_half))
        pdf = jnp.exp(-0.5 * u * u) * inv_root_two_pi
        act[rows_of(h), :] = (u * cdf).astype(jnp.bfloat16)
        grad = cot_v[rows_of(h), :].astype(jnp.float32) * (cdf + u * pdf)
        pg[rows_of(h), :] = grad.astype(jnp.bfloat16)

    def rs_len(d, h):
        return 4 if (h % 2 == 0) == (d == RIGHT) else 3

    def rs_copy(d, k, h):
        return pltpu.make_async_remote_copy(
            src_ref=rs_out.at[d, k - 1, rows_of(h)], dst_ref=rs_in.at[d, k - 1, rows_of(h)],
            send_sem=rs_send.at[d, k - 1, h], recv_sem=rs_recv.at[d, k - 1, h],
            device_id=(f, to_node(d, k - RS_TREE[k])), device_id_type=MESH,
        )

    def rs_add(total, d, k, h):
        for j in sorted(RS_TREE):
            if RS_TREE[j] == k and j <= rs_len(d, h):
                rs_copy(d, j, h).wait_recv()
                total = total + rs_in[d, j - 1, rows_of(h), :].astype(jnp.float32)
        return total

    def term(m, h):
        block = jnp.concatenate([adj[2 * m], adj[2 * m + 1]], axis=1)
        return dot(pg[rows_of(h), :], block, PLAIN)

    def rs_step(k, h):
        for d in (RIGHT, LEFT):
            if k > rs_len(d, h):
                continue
            total = rs_add(term(to_node(d, k), h), d, k, h)
            rs_out[d, k - 1, rows_of(h), :] = total.astype(jnp.bfloat16)
            copy = rs_copy(d, k, h)
            copy.start()
            finals.append(copy.wait_send)

    def rs_end(h):
        total = term(n, h)
        for d in (RIGHT, LEFT):
            total = rs_add(total, d, 0, h)
        ng[rows_of(h), :] = total.astype(jnp.bfloat16)

    def wg_copy(w, i):
        to = lax.rem(group + i, groups)
        return pltpu.make_async_remote_copy(
            src_ref=wg_out.at[w, to], dst_ref=wg_in.at[w, group],
            send_sem=wg_send.at[w], recv_sem=wg_recv.at[w],
            device_id=(feat_of(to, fz), n), device_id_type=MESH,
        )

    def wg_all(w):
        block = wg_in.at[w, pl.ds(0, groups - 1)]
        return pltpu.make_async_remote_copy(
            src_ref=block, dst_ref=block, send_sem=wg_send.at[w], recv_sem=wg_recv.at[w],
            device_id=(f, n), device_id_type=MESH,
        )

    def wg_start(w):
        units = pl.ds(w * 128, 128)
        rows = 2 * nz * part
        for q in range(groups // 2):
            features = pl.ds(q * rows, rows)
            block = dot(x[0, features, :], ng[units, pl.ds(0, half)], NEAR)
            block = block + dot(x[1, features, :], ng[units, pl.ds(half, half)], NEAR)
            block = block.astype(jnp.bfloat16).reshape(nz, 2, part, 128)
            for c in range(2):
                wg_out[w, 2 * q + c] = block[:, c]
        for i in range(1, groups):
            wg_copy(w, i).start()
        wg_in[w, group] = wg_out[w, group]

    def y_copy(w, i):
        z = lax.rem(fz + lax.rem(i, nz), nz)
        to = lax.rem(n + lax.div(i, nz), nn)
        return pltpu.make_async_remote_copy(
            src_ref=ys.at[w, z, to], dst_ref=y_in.at[w, fz * nn + n],
            send_sem=y_send.at[w], recv_sem=y_recv.at[w],
            device_id=(feat_of(group, z), to), device_id_type=MESH,
        )

    def y_all(w):
        block = y_in.at[w, pl.ds(0, nz * nn - 1)]
        return pltpu.make_async_remote_copy(
            src_ref=block, dst_ref=block, send_sem=y_send.at[w], recv_sem=y_recv.at[w],
            device_id=(f, n), device_id_type=MESH,
        )

    def wg_sum(w):
        wg_all(w).wait_recv()
        total = jnp.sum(wg_in[w].astype(jnp.float32), axis=0)
        for k in range(nn):
            ys[w, :, k] = total[:, 2 * k : 2 * k + 2]

        def send_y(i, carry):
            y_copy(w, i).start()
            return carry

        lax.fori_loop(1, nz * nn, send_y, 0)
        y_in[w, fz * nn + n] = ys[w, fz, n]

    def y_sum(w):
        y_all(w).wait_recv()
        wgrad[:, pl.ds(w * 128, 128)] = jnp.sum(y_in[w], axis=0)

    halves = range(NH)
    project(0)
    for k in ORDER[:2]:
        for h in halves:
            ag_step(k, 0, h)
    project(1)
    for h in halves:
        ag_step(ORDER[0], 1, h)
    for h in halves:
        ag_step(ORDER[2], 0, h)
    for h in halves:
        ag_step(ORDER[1], 1, h)
    for h in halves:
        ag_step(ORDER[3], 0, h)
    for h in halves:
        ag_step(ORDER[2], 1, h)
        ag_step(ORDER[3], 1, h)
        activate(h)
        for k in (4, 3):
            if k not in RS_TREE.values():
                rs_step(k, h)
    for k in (3, 2, 1):
        if k in RS_TREE.values() or k < 3:
            for h in halves:
                rs_step(k, h)
    for w in range(2):
        for h in range(w * NH // 2, (w + 1) * NH // 2):
            rs_end(h)
        wg_start(w)
    for w in range(2):
        wg_sum(w)
    for w in range(2):
        y_sum(w)
        wg_all(w).wait_send()
        y_all(w).wait_send()
    for a in range(2):
        all_feats(a).wait_send()
    for wait in finals:
        wait()


def per_device(nf, nn, feats, weight, tile_row, tile_col, tile_block, tile_count, edge_blocks, cotangent):
    fin, hid = weight.shape
    own = cotangent.shape[1]
    half = own // 2
    part = feats.shape[0]
    slots = edge_blocks.shape[2]
    bf, f32 = jnp.bfloat16, jnp.float32
    vm, dma = pltpu.VMEM, pltpu.SemaphoreType.DMA
    smem = pltpu.SMEM
    anywhere = pl.BlockSpec(memory_space=pltpu.HBM)
    return pl.pallas_call(
        functools.partial(kernel, nf, nn),
        out_shape=(
            jax.ShapeDtypeStruct((hid, own), bf),
            jax.ShapeDtypeStruct((fin // (nf * nn), hid), f32),
        ),
        in_specs=[anywhere] * 3 + [pl.BlockSpec(memory_space=smem)] + [anywhere] * 4,
        out_specs=(pl.BlockSpec(memory_space=vm), pl.BlockSpec(memory_space=vm)),
        scratch_shapes=[
            smem(tile_row.shape, jnp.int32),
            smem(tile_col.shape, jnp.int32),
            smem(tile_block.shape, jnp.int32),
            vm((slots, half, half), bf),
            vm((fin, hid), bf),
            vm((hid, own), bf),
            vm(feats.shape, bf),
            vm((2, nf, part, half), bf),
            vm((hid, fin), bf),
            vm((2 * nn, own, half), bf),
            vm((2, fin, half), bf),
            vm((nn, 2, hid, half), bf),
            vm((hid, own), f32),
            vm((hid, own), bf),
            vm((2, 4, hid, own), bf),
            vm((2, 4, hid, own), bf),
            vm((hid, own), bf),
            vm((2, nf // nn, nn, part, 128), bf),
            vm((2, nf // nn, nn, part, 128), bf),
            vm((2, nn, nn, 2, 128), f32),
            vm((2, nn * nn, 2, 128), f32),
            dma((7,)),
            dma((2,)),
            dma((2,)),
            dma((2, 4, 2, NH)),
            dma((2, 4, 2, NH)),
            dma((2, 4, NH)),
            dma((2, 4, NH)),
            dma((2,)),
            dma((2,)),
            dma((2,)),
            dma((2,)),
        ],
        compiler_params=pltpu.CompilerParams(
            collective_id=0, has_side_effects=True, vmem_limit_bytes=40 * 1024 * 1024
        ),
        name="graphconv",
    )(*[stay(v) for v in (tile_row, tile_col, tile_block)], tile_count, *[stay(v) for v in (feats, weight, edge_blocks, cotangent)])


def stay(array):
    return pltpu.with_memory_space_constraint(array, pltpu.HBM)


def solution(mesh):
    return jax.shard_map(
        functools.partial(per_device, mesh.shape["feat"], mesh.shape["node"]),
        mesh=mesh,
        in_specs=(
            P("feat", "node"),
            P(),
            P("feat", "node", None),
            P("feat", "node", None),
            P("feat", "node", None),
            P("feat", "node"),
            P("feat", "node", None, None, None),
            P(None, ("node", "feat")),
        ),
        out_specs=(P(None, ("node", "feat")), P(("feat", "node"), None)),
        check_vma=False,
    )
```

time: 86.7 us -> 78.3 us (0.903)
  local copies, waits for them, and re-layouts: 5.45 us -> 1.24 us
  Pallas kernels: 79.6 us -> 75.7 us
    unnamed x16 -> x2, local copies, waits for them, and re-layouts: 5.45 us -> 1.24 us
    pallas_call x1, Pallas kernels: 79.6 us -> 75.7 us  [per_device(): pl.pallas_call(functools.partial(kernel, nf, nn), out_shape=(jax.ShapeDty...]
where the time goes in v3:
time: 78.3 us; the launch traced here: 78.2 us
  Pallas kernels  75.7 us (97%)
  between operations  1.29 us (2%)
  local copies, waits for them, and re-layouts  1.24 us (2%)
    pallas_call x1, Pallas kernels, per_device(): pl.pallas_call(functools.partial(kernel, nf, nn), out_shape=(jax.ShapeDty...  75.7 us

profile of v3, /device:TPU:1, one launch (start us, length us, event | category | flops | bytes accessed | tf_op | source)
XLA Modules:
  0.0 78.2 jit_solution(10985341516491993533)
XLA Ops:
  1.3 75.7 %graphconv.1 = (bf16[256,256]{1,0:T(8,128)(2,1)S(1)}, f32[2,256]{1,0:T(2,128)S(1)}) custom-call(s32[1,1,32]{2,1,0:T(1,128)} %row_any.1, s32[1,1,32]{2,1,0:T(1,128)} %col_any.1, s32[1,1,32]{2,1,0:T(1,128)} %blk_any.1, s32[1,1]{1,0:T(1,128)S(6)} %copy.12.cnt_ref, bf16[16,16384]{1,0:T(8,128)(2,1)} %feats.1, bf16[1024,256]{1,0:T(8,128)(2,1)} %weight.1, ...), custom_call_target="tpu_custom_call" | custom-call | tf_op jit(solution)/shard_map/graphconv/pallas_call | solution.py:355
  77.0 0.7 copy.13
  77.6 0.6 copy.14

commit v4 on v3

--- a/solution.py
+++ b/solution.py
@@ -85,8 +85,7 @@
 
     pl.semaphore_wait(barrier, nf - 1 + nz * (nn - 1))
 
-    def feat_copy(a, i):
-        to = lax.rem(f + i, nf)
+    def feat_copy(a, to):
         return pltpu.make_async_remote_copy(
             src_ref=fs.at[a, to],
             dst_ref=x.at[a, pl.ds(pl.multiple_of(f * part, part), part)],
@@ -99,7 +98,7 @@
     for a in range(2):
 
         def send_feat(i, carry):
-            feat_copy(a, i).start()
+            feat_copy(a, lax.rem(f + i, nf)).start()
             return carry
 
         lax.fori_loop(1, nf, send_feat, 0)
@@ -158,8 +157,8 @@
             device_id=(f, to_node(d, hop)), device_id_type=MESH,
         )
 
-    def ag_pass(d, at, a, h):
-        for k in sorted(AG_TREE, reverse=True):
+    def ag_pass(d, at, a, h, chosen=(4, 3, 2, 1)):
+        for k in chosen:
             if AG_TREE[k] == at and k <= ag_len(d, a, h):
                 copy = ag_copy(d, at, k - at, a, h)
                 copy.start()
@@ -174,10 +173,15 @@
 
     def project(a):
         all_feats(a).wait_recv()
-        p[n, a] = dot(wt[...], x[a], PLAIN).astype(jnp.bfloat16)
+        for w in range(2):
+            rows = pl.ds(w * 128, 128)
+            p[n, a, rows, :] = dot(wt[rows, :], x[a], PLAIN).astype(jnp.bfloat16)
+            for h in range(w * NH // 2, (w + 1) * NH // 2):
+                for d in (RIGHT, LEFT):
+                    ag_pass(d, 0, a, h, (4, 3, 2))
         for h in range(NH):
             for d in (RIGHT, LEFT):
-                ag_pass(d, 0, a, h)
+                ag_pass(d, 0, a, h, (1,))
         for h in range(NH):
             add_block(n, a, h, a == 0)
 
@@ -268,19 +272,19 @@
             wg_copy(w, i).start()
         wg_in[w, group] = wg_out[w, group]
 
-    def y_copy(w, i):
+    def y_copy(i):
         z = lax.rem(fz + lax.rem(i, nz), nz)
         to = lax.rem(n + lax.div(i, nz), nn)
         return pltpu.make_async_remote_copy(
-            src_ref=ys.at[w, z, to], dst_ref=y_in.at[w, fz * nn + n],
-            send_sem=y_send.at[w], recv_sem=y_recv.at[w],
+            src_ref=ys.at[z, to], dst_ref=y_in.at[fz * nn + n],
+            send_sem=y_send.at[0], recv_sem=y_recv.at[0],
             device_id=(feat_of(group, z), to), device_id_type=MESH,
         )
 
-    def y_all(w):
-        block = y_in.at[w, pl.ds(0, nz * nn - 1)]
-        return pltpu.make_async_remote_copy(
-            src_ref=block, dst_ref=block, send_sem=y_send.at[w], recv_sem=y_recv.at[w],
+    def y_all():
+        block = y_in.at[pl.ds(0, nz * nn - 1)]
+        return pltpu.make_async_remote_copy(
+            src_ref=block, dst_ref=block, send_sem=y_send.at[0], recv_sem=y_recv.at[0],
             device_id=(f, n), device_id_type=MESH,
         )
 
@@ -288,18 +292,19 @@
         wg_all(w).wait_recv()
         total = jnp.sum(wg_in[w].astype(jnp.float32), axis=0)
         for k in range(nn):
-            ys[w, :, k] = total[:, 2 * k : 2 * k + 2]
-
+            ys[:, k, w] = total[:, 2 * k : 2 * k + 2]
+
+    def y_exchange():
         def send_y(i, carry):
-            y_copy(w, i).start()
+            y_copy(i).start()
             return carry
 
         lax.fori_loop(1, nz * nn, send_y, 0)
-        y_in[w, fz * nn + n] = ys[w, fz, n]
-
-    def y_sum(w):
-        y_all(w).wait_recv()
-        wgrad[:, pl.ds(w * 128, 128)] = jnp.sum(y_in[w], axis=0)
+        y_in[fz * nn + n] = ys[fz, n]
+        y_all().wait_recv()
+        total = jnp.sum(y_in[...], axis=0)
+        for w in range(2):
+            wgrad[:, pl.ds(w * 128, 128)] = total[w]
 
     halves = range(NH)
     project(0)
@@ -332,10 +337,10 @@
         wg_start(w)
     for w in range(2):
         wg_sum(w)
+    y_exchange()
     for w in range(2):
-        y_sum(w)
         wg_all(w).wait_send()
-        y_all(w).wait_send()
+    y_all().wait_send()
     for a in range(2):
         all_feats(a).wait_send()
     for wait in finals:
@@ -380,8 +385,8 @@
             vm((hid, own), bf),
             vm((2, nf // nn, nn, part, 128), bf),
             vm((2, nf // nn, nn, part, 128), bf),
-            vm((2, nn, nn, 2, 128), f32),
-            vm((2, nn * nn, 2, 128), f32),
+            vm((nn, nn, 2, 2, 128), f32),
+            vm((nn * nn, 2, 2, 128), f32),
             dma((7,)),
             dma((2,)),
             dma((2,)),

time: 78.3 us -> 77.3 us (0.987)
  Pallas kernels: 75.7 us -> 74.7 us
    pallas_call x1, Pallas kernels: 75.7 us -> 74.7 us  [per_device(): pl.pallas_call(functools.partial(kernel, nf, nn), out_shape=(jax.ShapeDty...]
where the time goes in v4:
time: 77.3 us; the launch traced here: 77.2 us
  Pallas kernels  74.7 us (97%)
  between operations  1.29 us (2%)
  local copies, waits for them, and re-layouts  1.24 us (2%)
    pallas_call x1, Pallas kernels, per_device(): pl.pallas_call(functools.partial(kernel, nf, nn), out_shape=(jax.ShapeDty...  74.7 us

profile of v4, /device:TPU:1, one launch (start us, length us, event | category | flops | bytes accessed | tf_op | source)
XLA Modules:
  0.0 77.2 jit_solution(2359185652183060672)
XLA Ops:
  1.3 74.7 %graphconv.1 = (bf16[256,256]{1,0:T(8,128)(2,1)S(1)}, f32[2,256]{1,0:T(2,128)S(1)}) custom-call(s32[1,1,32]{2,1,0:T(1,128)} %row_any.1, s32[1,1,32]{2,1,0:T(1,128)} %col_any.1, s32[1,1,32]{2,1,0:T(1,128)} %blk_any.1, s32[1,1]{1,0:T(1,128)S(6)} %copy.12.cnt_ref, bf16[16,16384]{1,0:T(8,128)(2,1)} %feats.1, bf16[1024,256]{1,0:T(8,128)(2,1)} %weight.1, ...), custom_call_target="tpu_custom_call" | custom-call | tf_op jit(solution)/shard_map/graphconv/pallas_call | solution.py:360
  76.0 0.7 copy.13
  76.6 0.6 copy.14

commit v5 on v4

--- a/solution.py
+++ b/solution.py
@@ -195,8 +195,11 @@
                 device_id=(f, n), device_id_type=MESH,
             ).wait_recv()
             ag_pass(d, k, a, h)
-        for d in got:
-            add_block(slot_at(d, k), a, h, False)
+
+    def ag_add(k, a, h):
+        for d in (RIGHT, LEFT):
+            if k <= ag_len(d, a, h):
+                add_block(slot_at(d, k), a, h, False)
 
     def activate(h):
         u = acc[rows_of(h), :]
@@ -311,18 +314,30 @@
     for k in ORDER[:2]:
         for h in halves:
             ag_step(k, 0, h)
+        for h in halves:
+            ag_add(k, 0, h)
     project(1)
     for h in halves:
         ag_step(ORDER[0], 1, h)
     for h in halves:
+        ag_add(ORDER[0], 1, h)
+    for h in halves:
         ag_step(ORDER[2], 0, h)
     for h in halves:
+        ag_add(ORDER[2], 0, h)
+    for h in halves:
         ag_step(ORDER[1], 1, h)
     for h in halves:
+        ag_add(ORDER[1], 1, h)
+    for h in halves:
         ag_step(ORDER[3], 0, h)
+    for h in halves:
+        ag_add(ORDER[3], 0, h)
     for h in halves:
         ag_step(ORDER[2], 1, h)
         ag_step(ORDER[3], 1, h)
+        ag_add(ORDER[2], 1, h)
+        ag_add(ORDER[3], 1, h)
         activate(h)
         for k in (4, 3):
             if k not in RS_TREE.values():

time: 77.3 us -> 77.6 us (level)
  no operation moved by 1% of the time
where the time goes in v5:
time: 77.6 us; the launch traced here: 77.5 us
  Pallas kernels  75 us (97%)
  between operations  1.29 us (2%)
  local copies, waits for them, and re-layouts  1.24 us (2%)
    pallas_call x1, Pallas kernels, per_device(): pl.pallas_call(functools.partial(kernel, nf, nn), out_shape=(jax.ShapeDty...  75 us

profile of v5, /device:TPU:1, one launch (start us, length us, event | category | flops | bytes accessed | tf_op | source)
XLA Modules:
  0.0 77.5 jit_solution(17941925586732907621)
XLA Ops:
  1.3 75.0 %graphconv.1 = (bf16[256,256]{1,0:T(8,128)(2,1)S(1)}, f32[2,256]{1,0:T(2,128)S(1)}) custom-call(s32[1,1,32]{2,1,0:T(1,128)} %row_any.1, s32[1,1,32]{2,1,0:T(1,128)} %col_any.1, s32[1,1,32]{2,1,0:T(1,128)} %blk_any.1, s32[1,1]{1,0:T(1,128)S(6)} %copy.12.cnt_ref, bf16[16,16384]{1,0:T(8,128)(2,1)} %feats.1, bf16[1024,256]{1,0:T(8,128)(2,1)} %weight.1, ...), custom_call_target="tpu_custom_call" | custom-call | tf_op jit(solution)/shard_map/graphconv/pallas_call | solution.py:375
  76.2 0.7 copy.13
  76.9 0.6 copy.14
